TPU v7x, 512 devices: a whole 4x4x16 slice. The times are simulated.
512 devices in a mesh: row: 64 (over z, y), col: 8 (over x, core).
Axes of the slice: x: 4, y: 4, z: 16, core: 2. Of those that a mesh axis runs over, the one named last changes fastest.
Arguments:
- amplitudes: bfloat16 [2048, 16384], P('row', 'col'), may hold values from -6 to 6
- integrals: bfloat16 [2048, 16384], P('col', 'row'), may hold values from -0.125 to 0.125
- amp_mask: int32 [64, 128], replicated, may hold values 0 or 1
- int_mask: int32 [64, 128], replicated, may hold values 0 or 1
Outputs:
- scaled_residual: float32 [16384, 16384], P('col', 'row')
- row_norm: float32 [16384], P('col')
Inputs may be any that keep to these rules, and one draw needn't show every extreme that they name: `amp_mask`: an entry of 1 keeps its tile, 0 drops it. `int_mask`: an entry of 1 keeps its tile, 0 drops it.
All inputs are finite; a program needn't handle non-finite values.
Results may differ from a plain program's by a relative error of at most 0.0003.
Values may be sent and summed in bfloat16 or wider, within the bound.
A program may use at most 64 MiB of HBM per device.

v0:
```python
import jax
import jax.numpy as jnp
from jax import lax
from jax.sharding import PartitionSpec as P

OCC = 128
TILE = 128


def contract(left, right):
    return lax.dot_general(
        left, right, (((0,), (0,)), ((), ())), preferred_element_type=jnp.float32
    )


def row_keep(table, start, count, block):
    blocks = table.shape[0]
    owners = (start + jnp.arange(count, dtype=jnp.int32)) // block
    onehot = (owners[:, None] == jnp.arange(blocks, dtype=jnp.int32)[None, :]).astype(jnp.bfloat16)
    picked = jnp.dot(onehot, table.astype(jnp.bfloat16), preferred_element_type=jnp.float32)
    return jnp.repeat(picked, TILE, axis=1).astype(jnp.bfloat16)


def local(amplitudes, integrals, amp_mask, int_mask):
    block, m_dev = amplitudes.shape
    ab_dev = integrals.shape[1]
    row_place = lax.axis_index("row")
    col_place = lax.axis_index("col")
    m_tiles = m_dev // TILE
    n_tiles = ab_dev // TILE
    occ_dev = m_dev // OCC
    amp_keep = lax.dynamic_slice_in_dim(amp_mask, col_place * m_tiles, m_tiles, 1)
    int_keep = lax.dynamic_slice_in_dim(int_mask, row_place * n_tiles, n_tiles, 1)
    own_amp = amplitudes * row_keep(amp_keep, row_place * block, block, block)
    stacked = own_amp[None]
    whole_int = lax.all_gather(integrals, "col", axis=0, tiled=True)
    whole_int = whole_int * row_keep(int_keep, 0, whole_int.shape[0], block)
    total = contract(lax.all_gather(stacked, "row", axis=1, tiled=True)[0], whole_int)
    cube = total.reshape(occ_dev, OCC, ab_dev)
    moved = lax.all_to_all(cube, "col", split_axis=1, concat_axis=0, tiled=True)
    mirror = moved.transpose(1, 0, 2).reshape(m_dev, ab_dev)
    summed = total + mirror
    squares = lax.psum(jnp.sum(summed * summed, axis=1), "row")
    row_norm = jnp.sqrt(squares / (ab_dev * lax.axis_size("row")) + 1e-06)
    return (summed / row_norm[:, None], row_norm)


def solution(mesh):
    return jax.shard_map(
        local,
        mesh=mesh,
        in_specs=(P("row", "col"), P("col", "row"), P(), P()),
        out_specs=(P("col", "row"), P("col")),
        check_vma=False,
    )
```

profile of v0, /device:TPU:2, one launch (start us, length us, event | category | flops | bytes accessed | tf_op | source)
XLA Modules:
  0.0 403.9 jit_solution(1154354201146444259)
XLA Ops:
  7.2 0.0 all-gather.4.cloned.1.call-start
  7.2 0.7 all-gather.4.cloned.1.call-update
  7.9 0.0 all-gather.6.cloned.1.call-start
  8.0 1.0 convolution_convert_fusion.1
  9.0 0.1 copy.9
  9.1 0.1 broadcast_in_dim.6
  9.2 1.6 bitcast_multiply_fusion.2
  10.8 0.0 all-gather.6.cloned.1.call-update
  10.9 1.3 convolution_convert_fusion
  12.1 0.3 copy.10
  12.4 31.8 %all-gather.4.cloned.1.call-done = bf16[2048,256]{1,0:T(8,128)(2,1)} async-done(((bf16[256,256]{1,0:T(8,128)(2,1)}), bf16[2048,256]{1,0:T(8,128)(2,1)}) %all-gather.4.cloned.1.call-update) | async-done | bytes 1048592 | tf_op jit(solution)/shard_map/all_gather | solution.py:36
  44.2 160.9 %all-gather.6.cloned.1.call-done = bf16[2048,2048]{1,0:T(8,128)(2,1)} async-done(((bf16[32,2048]{1,0:T(8,128)(2,1)}), bf16[2048,2048]{1,0:T(8,128)(2,1)}) %all-gather.6.cloned.1.call-update) | async-done | bytes 8388624 | tf_op jit(solution)/shard_map/all_gather | solution.py:38
  205.1 5.8 %broadcast_in_dim.16 = bf16[2048,2,128]{2,1,0:T(2,128)(2,1)S(1)} broadcast(bf16[2048,2]{1,0:T(8,128)(2,1)S(1)} %copy.10), dimensions={0,1} | broadcast | bytes 1056768 | tf_op jit(solution)/shard_map/broadcast_in_dim | solution.py:21
  210.9 6.1 %fusion = f32[2048,256]{1,0:T(8,128)S(1)} fusion(bf16[2048,2048]{1,0:T(8,128)(2,1)} %all-gather.6.cloned.1.call-done, bf16[2048,256]{1,0:T(8,128)(2,1)} %all-gather.4.cloned.1.call-done, bf16[256,8,2,128]{3,2,1,0:T(2,128)(2,1)S(1)} %bitcast.24), kind=kOutput, calls=%fused_computation.5 | convolution fusion | flops 2148007936 | bytes 12582912 | tf_op jit(solution)/shard_map/dot_general | solution.py:11
  217.0 1.2 copy.11
  218.3 30.6 %all_to_all.18 = f32[16,128,256]{2,0,1:T(8,128)S(1)} all-to-all(f32[16,128,256]{2,0,1:T(8,128)S(1)} %copy.11), channel_id=1, replica_groups=mesh['row'=64,'col'=8] {'col'}, dimensions={1} | all-to-all | bytes 4194304 | tf_op jit(solution)/shard_map/all_to_all | solution.py:40
  248.8 0.2 copy.12
  249.0 0.0 copy-start
  249.0 1.3 copy-done
  250.4 0.4 multiply_reduce_fusion
  250.8 142.9 %psum.7 = f32[2048]{0:T(1024)S(1)} all-reduce(f32[2048]{0:T(1024)S(1)} %multiply_reduce_fusion), channel_id=1, replica_groups=mesh['row'=64,'col'=8] {'row'}, use_global_device_ids=true, to_apply=%region_1.2 | all-reduce | flops 2048 | bytes 16384 | tf_op jit(solution)/shard_map/psum | solution.py:43
  393.8 0.0 copy-start.1
  393.8 3.3 broadcast_divide_fusion
  397.0 0.0 copy-done.1
  (3 shorter events, 0.0 us)
Async XLA Ops:
  7.2 37.0 %all-gather.4.cloned.1.call-start = ((), (), s32[]{:S(2)}) async-start(), calls=%async_computation.1 | async-start | bytes 1179648 | tf_op jit(solution)/shard_map/all_gather | solution.py:36
  7.9 197.2 %all-gather.6.cloned.1.call-start = ((), (), s32[]{:S(2)}) async-start(), calls=%async_computation.2 | async-start | bytes 8519680 | tf_op jit(solution)/shard_map/all_gather | solution.py:38
  249.0 1.3 copy-start
  393.8 3.3 copy-start.1
Sparse Core Ops, SparseCore 0:
  10.1 34.0 all-gather.3
  47.7 157.3 all-gather.5
where the time goes:
time: 404 us
  waiting for transfers between devices  193 us (48%)
  blocking collectives  174 us (43%)
  between operations  14.1 us (3%)
  local copies, waits for them, and re-layouts  9.05 us (2%)
  matrix products  8.42 us (2%)
  other arithmetic  5.29 us (1%)
    all_gather x1, waiting for transfers between devices, local(): lax.all_gather(stacked, 'row', axis=1, tiled=True)[0]  161 us
    psum x1, blocking collectives, local(): squares = lax.psum(jnp.sum(summed * summed, axis=1), 'row')  143 us
    all_gather x1, waiting for transfers between devices, local(): whole_int = lax.all_gather(integrals, 'col', axis=0, tiled=True)  31.8 us
    all_to_all x1, blocking collectives, local(): moved = lax.all_to_all(cube, 'col', split_axis=1, concat_axis=0, tiled=True)  30.6 us
  transfers between devices with their start and end apart: 2, of which 2 were waited for; matrix products, arithmetic and copies ran while one was open for 1% of the time, Pallas kernels for 0%

commit v1 on v0

v1 whole, which is shorter than its diff:
```python
import functools

import jax
import jax.numpy as jnp
from jax import lax
from jax.experimental import pallas as pl
from jax.experimental.pallas import tpu as pltpu
from jax.sharding import PartitionSpec as P

TILE = 128
OCC = 128
Y = 4
H = 2
MESH = pl.DeviceIdType.MESH
WIDTH = 16384


def kernel(
    nz, nc, am_ref, bm_ref, a_ref, b_ref, s_ref, n_ref,
    A, B, L, R, NZ, NY,
    loc_sem,
    pz_s, pz_r, qz_s, qz_r, py_s, py_r, qy_s, qy_r,
    b_s, b_r, x_s, x_r, nz_s, nz_r, ny_s, ny_r,
):
    kb, m_dev = a_ref.shape
    kc, n_dev = b_ref.shape
    mh = m_dev // H
    cp = (mh * 5 // 8) // TILE * TILE
    half = kb // 2
    bun = Y * kb
    occ = m_dev // OCC
    oh = occ // H
    far = nz // 2
    r = lax.axis_index("row")
    c = lax.axis_index("col")
    z = r // Y
    y = r % Y

    def at_z(d):
        return (lax.rem(z + d + 2 * nz, nz) * Y + y, c)

    def at_y(d):
        return (z * Y + lax.rem(y + d + 2 * Y, Y), c)

    def at_c(k):
        return (r, lax.rem(c + k, nc))

    def remote(src, dst, ss, rs, dev):
        return pltpu.make_async_remote_copy(
            src_ref=src, dst_ref=dst, send_sem=ss, recv_sem=rs,
            device_id=dev, device_id_type=MESH,
        )

    for t in range(m_dev // TILE):
        keep = am_ref[r, c * (m_dev // TILE) + t].astype(jnp.float32)
        lo = t * TILE
        val = (a_ref[:, lo:lo + TILE].astype(jnp.float32) * keep).astype(jnp.bfloat16)
        A[lo // mh, pl.ds(pl.multiple_of(r * kb, kb), kb), lo % mh:lo % mh + TILE] = val
    for u in range(kc // kb):
        for t in range(n_dev // TILE):
            keep = bm_ref[c * (kc // kb) + u, r * (n_dev // TILE) + t].astype(jnp.float32)
            val = b_ref[u * kb:(u + 1) * kb, t * TILE:(t + 1) * TILE].astype(jnp.float32) * keep
            B[pl.ds(pl.multiple_of(c * kc + u * kb, kb), kb), t * TILE:(t + 1) * TILE] = val.astype(jnp.bfloat16)

    barrier = pltpu.get_barrier_semaphore()
    for k in range(1, nz):
        pl.semaphore_signal(barrier, inc=1, device_id=at_z(k), device_id_type=MESH)
    for k in range(1, Y):
        pl.semaphore_signal(barrier, inc=1, device_id=at_y(k), device_id_type=MESH)
    for k in range(1, nc):
        pl.semaphore_signal(barrier, inc=1, device_id=at_c(k), device_id_type=MESH)
    pl.semaphore_wait(barrier, nz - 1 + Y - 1 + nc - 1)

    def block(h, dz, dy, first, rows):
        zz = lax.rem(z + dz + 2 * nz, nz)
        yy = lax.rem(y + dy + 2 * Y, Y)
        return A.at[h, pl.ds(pl.multiple_of((zz * Y + yy) * kb + first, half), rows), :cp]

    def bundle(h, dz, first, rows):
        zz = lax.rem(z + dz + 2 * nz, nz)
        return A.at[h, pl.ds(pl.multiple_of(zz * bun + first, half), rows), cp:]

    sign = (1, -1)

    def pz(h, d, s, back, last):
        ref = block(h, -sign[d] * (s - 1 + back), 0, d * half if last else 0, half if last else kb)
        return remote(ref, ref, pz_s.at[h, d, s], pz_r.at[h, d, s], at_z(sign[d]))

    def qz(h, d, s, back, last):
        ref = bundle(h, -sign[d] * (s - 1 + back), d * (bun // 2) if last else 0, bun // 2 if last else bun)
        return remote(ref, ref, qz_s.at[h, d, s], qz_r.at[h, d, s], at_z(sign[d]))

    def py(h, slot, dz, kind, back):
        d = kind % 2
        whole = kind < 2
        dy = -sign[d] * ((0 if whole else 1) + back)
        ref = block(h, dz, dy, 0 if whole else d * half, kb if whole else half)
        return remote(ref, ref, py_s.at[h, slot, kind], py_r.at[h, slot, kind], at_y(sign[d]))

    def qy(h, k, back):
        yy = lax.rem(y - back * k + 2 * Y, Y)
        ref = A.at[h, pl.ds(pl.multiple_of((z * Y + yy) * kb, kb), kb), cp:]
        return remote(ref, ref, qy_s.at[h, k], qy_r.at[h, k], at_y(k))

    def slot_of(d, s):
        return s if d == 0 else far + s

    def spread(h, slot, dz):
        py(h, slot, dz, 0, 0).start()
        py(h, slot, dz, 1, 0).start()

    def relay(h, slot, dz):
        py(h, slot, dz, 0, 1).wait_recv()
        py(h, slot, dz, 2, 0).start()
        py(h, slot, dz, 1, 1).wait_recv()
        py(h, slot, dz, 3, 0).start()

    def begin(h):
        for k in (1, 3, 2):
            qy(h, k, 0).start()
        for d in range(2):
            pz(h, d, 1, 0, False).start()
        spread(h, 0, 0)

    def step(h, s, first=False, last=False):
        for d in range(2):
            pz(h, d, s, 1, False).wait_recv()
            pz(h, d, s + 1, 0, last).start()
            spread(h, slot_of(d, s), -sign[d] * s)
        if first:
            relay(h, 0, 0)
        else:
            for d in range(2):
                relay(h, slot_of(d, s - 1), -sign[d] * (s - 1))
        for d in range(2):
            qz(h, d, s, 1, False).wait_recv()
            qz(h, d, s + 1, 0, last).start()

    def gather(h):
        for k in (1, 3, 2):
            qy(h, k, 1).wait_recv()
        for d in range(2):
            qz(h, d, 1, 0, False).start()
        step(h, 1, first=True)

        def body(s, carry):
            step(h, s)
            return carry

        lax.fori_loop(2, far - 1, body, 0)
        step(h, far - 1, last=True)
        for d in range(2):
            pz(h, d, far, 1, True).wait_recv()
        spread(h, far, far)
        for d in range(2):
            relay(h, slot_of(d, far - 1), -sign[d] * (far - 1))
        if h + 1 < H:
            begin(h + 1)
        for d in range(2):
            qz(h, d, far, 1, True).wait_recv()
        relay(h, far, far)

        def rest(i, carry):
            dz = jnp.where(i <= far, -i, i - far)
            for kind in (2, 3):
                py(h, i, dz, kind, 1).wait_recv()
            return carry

        lax.fori_loop(0, nz, rest, 0)

    def b_copy(k, back):
        src = lax.rem(c - back * k + nc, nc)
        ref = B.at[pl.ds(pl.multiple_of(src * kc, kc), kc), :]
        return remote(ref, ref, b_s.at[k], b_r.at[k], at_c(k))

    def x_copy(h, k, back):
        to = lax.rem(c + (1 - back) * k, nc)
        src = lax.rem(c - back * k + nc, nc)
        return remote(
            L.at[pl.ds(h * oh, oh), pl.ds(pl.multiple_of(to * occ, occ), occ), :],
            R.at[src, pl.ds(h * oh, oh)],
            x_s.at[h, k], x_r.at[h, k], at_c(k),
        )

    def n_copy(buf, ss, rs, me, k, n, dev, back):
        ref = buf.at[lax.rem(me - back * k + n, n)]
        return remote(ref, ref, ss.at[k], rs.at[k], dev)

    begin(0)
    for k in range(1, nc):
        b_copy(k, 0).start()
    for h in range(H):
        gather(h)
        if h == 0:
            for k in range(1, nc):
                b_copy(k, 1).wait_recv()

        def product(i, carry):
            cols = pl.ds(pl.multiple_of(i * 2 * OCC, 2 * OCC), 2 * OCC)
            part = lax.dot_general(
                A[h, :, cols], B[...], (((0,), (0,)), ((), ())), preferred_element_type=jnp.float32
            )
            L[pl.ds(h * oh + 2 * i, 2)] = part.reshape(2, OCC, n_dev)
            return carry

        lax.fori_loop(0, oh // 2, product, 0)
        for k in range(1, nc):
            x_copy(h, k, 0).start()
        own = pltpu.make_async_copy(
            L.at[pl.ds(h * oh, oh), pl.ds(pl.multiple_of(c * occ, occ), occ), :],
            R.at[c, pl.ds(h * oh, oh)],
            loc_sem.at[h],
        )
        own.start()
        own.wait()

    for h in range(H):
        for k in range(1, nc):
            x_copy(h, k, 1).wait_recv()

        def add(src, carry):
            for o in range(0, oh, 8):
                got = jnp.swapaxes(R[src, pl.ds(h * oh + o, 8)], 0, 1)
                at = pl.ds(pl.multiple_of(src * occ + h * oh + o, 8), 8)
                s_ref[:, at, :] = L[:, at, :] + got
            return carry

        lax.fori_loop(0, nc, add, 0)

    def squares(i, carry):
        v = s_ref[i]
        v = v * v
        t = v[:, :TILE]
        for q in range(1, n_dev // TILE):
            t = t + v[:, q * TILE:(q + 1) * TILE]
        NZ[z, pl.ds(i, 1), :] = jnp.sum(t.T, axis=0, keepdims=True)
        return carry

    lax.fori_loop(0, occ, squares, 0)
    for k in range(1, nz):
        n_copy(NZ, nz_s, nz_r, z, k, nz, at_z(k), 0).start()
    for k in range(1, nz):
        n_copy(NZ, nz_s, nz_r, z, k, nz, at_z(k), 1).wait_recv()
    total = NZ[0]
    for q in range(1, nz):
        total = total + NZ[q]
    NY[y] = total
    for k in range(1, Y):
        n_copy(NY, ny_s, ny_r, y, k, Y, at_y(k), 0).start()
    for k in range(1, Y):
        n_copy(NY, ny_s, ny_r, y, k, Y, at_y(k), 1).wait_recv()
    total = NY[0]
    for q in range(1, Y):
        total = total + NY[q]
    n_ref[...] = jnp.sqrt(total / WIDTH + 1e-06)

    for h in range(H):
        for d in range(2):
            def sent(s, carry):
                pz(h, d, s, 0, False).wait_send()
                qz(h, d, s, 0, False).wait_send()
                return carry

            lax.fori_loop(1, far, sent, 0)
            pz(h, d, far, 0, True).wait_send()
            qz(h, d, far, 0, True).wait_send()

        def sent_y(i, carry):
            dz = jnp.where(i <= far, -i, i - far)
            for kind in range(4):
                py(h, i, dz, kind, 0).wait_send()
            return carry

        lax.fori_loop(0, nz, sent_y, 0)
        for k in range(1, Y):
            qy(h, k, 0).wait_send()
        for k in range(1, nc):
            x_copy(h, k, 0).wait_send()
    for k in range(1, nc):
        b_copy(k, 0).wait_send()
    for k in range(1, nz):
        n_copy(NZ, nz_s, nz_r, z, k, nz, at_z(k), 0).wait_send()
    for k in range(1, Y):
        n_copy(NY, ny_s, ny_r, y, k, Y, at_y(k), 0).wait_send()


def local(nrow, nc, amplitudes, integrals, amp_mask, int_mask):
    kb, m_dev = amplitudes.shape
    kc, n_dev = integrals.shape
    nz = nrow // Y
    k_all = kb * nrow
    occ = m_dev // OCC
    far = nz // 2
    dma = pltpu.SemaphoreType.DMA
    pairs = [(H, 2, far + 1), (H, 2, far + 1), (H, nz, 4), (H, Y), (nc,), (H, nc), (nz,), (Y,)]
    summed, norm = pl.pallas_call(
        functools.partial(kernel, nz, nc),
        out_shape=(
            jax.ShapeDtypeStruct((occ, OCC, n_dev), jnp.float32),
            jax.ShapeDtypeStruct((occ, OCC), jnp.float32),
        ),
        in_specs=[
            pl.BlockSpec(memory_space=pltpu.SMEM),
            pl.BlockSpec(memory_space=pltpu.SMEM),
            pl.BlockSpec(memory_space=pltpu.VMEM),
            pl.BlockSpec(memory_space=pltpu.VMEM),
        ],
        out_specs=(
            pl.BlockSpec(memory_space=pltpu.VMEM),
            pl.BlockSpec(memory_space=pltpu.VMEM),
        ),
        scratch_shapes=[
            pltpu.VMEM((H, k_all, m_dev // H), jnp.bfloat16),
            pltpu.VMEM((k_all, n_dev), jnp.bfloat16),
            pltpu.VMEM((occ, OCC, n_dev), jnp.float32),
            pltpu.VMEM((nc, occ, occ, n_dev), jnp.float32),
            pltpu.VMEM((nz, occ, OCC), jnp.float32),
            pltpu.VMEM((Y, occ, OCC), jnp.float32),
            dma((H,)),
        ] + [dma(p) for p in pairs for _ in range(2)],
        compiler_params=pltpu.CompilerParams(
            collective_id=0, has_side_effects=True, vmem_limit_bytes=40 << 20,
        ),
    )(amp_mask, int_mask, amplitudes, integrals)
    return summed.reshape(m_dev, n_dev) / norm.reshape(m_dev)[:, None], norm.reshape(m_dev)


def solution(mesh):
    return jax.shard_map(
        functools.partial(local, mesh.shape["row"], mesh.shape["col"]),
        mesh=mesh,
        in_specs=(P("row", "col"), P("col", "row"), P(), P()),
        out_specs=(P("col", "row"), P("col")),
        check_vma=False,
    )
```

time: 404 us -> 137 us (0.34)
  the two profiles are of different devices: /device:TPU:2 before, /device:TPU:1 now
where the time goes in v1:
time: 137 us
  Pallas kernels  130 us (95%)
  local copies, waits for them, and re-layouts  3.91 us (3%)
  other arithmetic  1.66 us (1%)
    pallas_call x1, Pallas kernels, local(): pl.pallas_call(functools.partial(kernel, nz, nc), out_shape=(jax.ShapeDty...  130 us
    unnamed x9, local copies, waits for them, and re-layouts  3.91 us

profile of v1, /device:TPU:1, one launch (start us, length us, event | category | flops | bytes accessed | tf_op | source)
XLA Modules:
  0.0 136.6 jit_solution(3917415728587069997)
XLA Ops:
  0.6 0.0 copy-start
  0.6 0.9 copy-done
  1.5 0.0 copy-start.1
  1.5 0.9 copy-done.1
  2.4 0.0 copy-start.2
  2.4 0.8 copy-done.2
  3.2 0.0 copy-start.3
  3.2 0.8 copy-done.3
  4.0 130.4 %shard_map.59 = (f32[16,128,256]{2,1,0:T(8,128)S(1)}, f32[16,128]{1,0:T(8,128)S(1)}) custom-call(s32[64,128]{1,0:T(8,128)S(1)} %copy-done.2, s32[64,128]{1,0:T(8,128)S(1)} %copy-done.3, bf16[32,2048]{1,0:T(8,128)(2,1)S(1)} %copy-done, bf16[256,256]{1,0:T(8,128)(2,1)S(1)} %copy-done.1), custom_call_target="tpu_custom_call" | custom-call | tf_op jit(solution)/shard_map/pallas_call | solution.py:296
  134.3 1.7 %bitcast_divide_fusion = f32[2048,256]{1,0:T(8,128)} fusion(f32[16,128,256]{2,1,0:T(8,128)S(1)} %get-tuple-element.4, f32[2048]{0:T(1024)S(1)} %bitcast.3), kind=kLoop, calls=%fused_computation | loop fusion | flops 524288 | bytes 4202496 | tf_op jit(solution)/shard_map/div | solution.py:325
  136.0 0.6 copy.7
Async XLA Ops:
  0.6 0.9 copy-start
  1.5 0.9 copy-start.1
  2.4 0.8 copy-start.2
  3.2 0.8 copy-start.3

commit v2 on v1

--- a/solution.py
+++ b/solution.py
@@ -18,6 +18,7 @@
 def kernel(
     nz, nc, am_ref, bm_ref, a_ref, b_ref, s_ref, n_ref,
     A, B, L, R, NZ, NY,
+    a_own, b_own, am_own, bm_own, in_sem,
     loc_sem,
     pz_s, pz_r, qz_s, qz_r, py_s, py_r, qy_s, qy_r,
     b_s, b_r, x_s, x_r, nz_s, nz_r, ny_s, ny_r,
@@ -27,7 +28,6 @@
     mh = m_dev // H
     cp = (mh * 5 // 8) // TILE * TILE
     half = kb // 2
-    bun = Y * kb
     occ = m_dev // OCC
     oh = occ // H
     far = nz // 2
@@ -51,16 +51,14 @@
             device_id=dev, device_id_type=MESH,
         )
 
-    for t in range(m_dev // TILE):
-        keep = am_ref[r, c * (m_dev // TILE) + t].astype(jnp.float32)
-        lo = t * TILE
-        val = (a_ref[:, lo:lo + TILE].astype(jnp.float32) * keep).astype(jnp.bfloat16)
-        A[lo // mh, pl.ds(pl.multiple_of(r * kb, kb), kb), lo % mh:lo % mh + TILE] = val
-    for u in range(kc // kb):
-        for t in range(n_dev // TILE):
-            keep = bm_ref[c * (kc // kb) + u, r * (n_dev // TILE) + t].astype(jnp.float32)
-            val = b_ref[u * kb:(u + 1) * kb, t * TILE:(t + 1) * TILE].astype(jnp.float32) * keep
-            B[pl.ds(pl.multiple_of(c * kc + u * kb, kb), kb), t * TILE:(t + 1) * TILE] = val.astype(jnp.bfloat16)
+    loads = (
+        pltpu.make_async_copy(am_ref.at[pl.ds(pl.multiple_of(r // 8 * 8, 8), 8)], am_own, in_sem.at[0]),
+        pltpu.make_async_copy(bm_ref.at[pl.ds(pl.multiple_of(c * (kc // kb), kc // kb), kc // kb)], bm_own, in_sem.at[1]),
+        pltpu.make_async_copy(a_ref, a_own, in_sem.at[2]),
+        pltpu.make_async_copy(b_ref, b_own, in_sem.at[3]),
+    )
+    for load in loads:
+        load.start()
 
     barrier = pltpu.get_barrier_semaphore()
     for k in range(1, nz):
@@ -69,6 +67,19 @@
         pl.semaphore_signal(barrier, inc=1, device_id=at_y(k), device_id_type=MESH)
     for k in range(1, nc):
         pl.semaphore_signal(barrier, inc=1, device_id=at_c(k), device_id_type=MESH)
+
+    for load in loads:
+        load.wait()
+    for t in range(m_dev // TILE):
+        keep = am_own[r % 8, c * (m_dev // TILE) + t].astype(jnp.float32)
+        lo = t * TILE
+        val = (a_own[:, lo:lo + TILE].astype(jnp.float32) * keep).astype(jnp.bfloat16)
+        A[lo // mh, pl.ds(pl.multiple_of(r * kb, kb), kb), lo % mh:lo % mh + TILE] = val
+    for u in range(kc // kb):
+        for t in range(n_dev // TILE):
+            keep = bm_own[u, r * (n_dev // TILE) + t].astype(jnp.float32)
+            val = b_own[u * kb:(u + 1) * kb, t * TILE:(t + 1) * TILE].astype(jnp.float32) * keep
+            B[pl.ds(pl.multiple_of(c * kc + u * kb, kb), kb), t * TILE:(t + 1) * TILE] = val.astype(jnp.bfloat16)
     pl.semaphore_wait(barrier, nz - 1 + Y - 1 + nc - 1)
 
     def block(h, dz, dy, first, rows):
@@ -76,9 +87,10 @@
         yy = lax.rem(y + dy + 2 * Y, Y)
         return A.at[h, pl.ds(pl.multiple_of((zz * Y + yy) * kb + first, half), rows), :cp]
 
-    def bundle(h, dz, first, rows):
+    def rest_of(h, dz, dy, first, rows):
         zz = lax.rem(z + dz + 2 * nz, nz)
-        return A.at[h, pl.ds(pl.multiple_of(zz * bun + first, half), rows), cp:]
+        yy = lax.rem(y + dy + 2 * Y, Y)
+        return A.at[h, pl.ds(pl.multiple_of((zz * Y + yy) * kb + first, half), rows), cp:]
 
     sign = (1, -1)
 
@@ -86,9 +98,9 @@
         ref = block(h, -sign[d] * (s - 1 + back), 0, d * half if last else 0, half if last else kb)
         return remote(ref, ref, pz_s.at[h, d, s], pz_r.at[h, d, s], at_z(sign[d]))
 
-    def qz(h, d, s, back, last):
-        ref = bundle(h, -sign[d] * (s - 1 + back), d * (bun // 2) if last else 0, bun // 2 if last else bun)
-        return remote(ref, ref, qz_s.at[h, d, s], qz_r.at[h, d, s], at_z(sign[d]))
+    def qz(h, d, s, e, back, last):
+        ref = rest_of(h, -sign[d] * (s - 1 + back), e, d * half if last else 0, half if last else kb)
+        return remote(ref, ref, qz_s.at[h, d, s, e], qz_r.at[h, d, s, e], at_z(sign[d]))
 
     def py(h, slot, dz, kind, back):
         d = kind % 2
@@ -98,8 +110,7 @@
         return remote(ref, ref, py_s.at[h, slot, kind], py_r.at[h, slot, kind], at_y(sign[d]))
 
     def qy(h, k, back):
-        yy = lax.rem(y - back * k + 2 * Y, Y)
-        ref = A.at[h, pl.ds(pl.multiple_of((z * Y + yy) * kb, kb), kb), cp:]
+        ref = rest_of(h, 0, -back * k, 0, kb)
         return remote(ref, ref, qy_s.at[h, k], qy_r.at[h, k], at_y(k))
 
     def slot_of(d, s):
@@ -115,49 +126,57 @@
         py(h, slot, dz, 1, 1).wait_recv()
         py(h, slot, dz, 3, 0).start()
 
+    order = (0, 3, 1, 2)
+
     def begin(h):
         for k in (1, 3, 2):
             qy(h, k, 0).start()
         for d in range(2):
             pz(h, d, 1, 0, False).start()
         spread(h, 0, 0)
+        for d in range(2):
+            qz(h, d, 1, 0, 0, False).start()
+
+    def join(h):
+        for k in (1, 3, 2):
+            qy(h, k, 1).wait_recv()
+            for d in range(2):
+                qz(h, d, 1, Y - k, 0, False).start()
 
     def step(h, s, first=False, last=False):
         for d in range(2):
             pz(h, d, s, 1, False).wait_recv()
             pz(h, d, s + 1, 0, last).start()
             spread(h, slot_of(d, s), -sign[d] * s)
-        if first:
-            relay(h, 0, 0)
-        else:
+        for n, e in enumerate(order):
+            if n == 2:
+                if first:
+                    relay(h, 0, 0)
+                else:
+                    for d in range(2):
+                        relay(h, slot_of(d, s - 1), -sign[d] * (s - 1))
             for d in range(2):
-                relay(h, slot_of(d, s - 1), -sign[d] * (s - 1))
-        for d in range(2):
-            qz(h, d, s, 1, False).wait_recv()
-            qz(h, d, s + 1, 0, last).start()
-
-    def gather(h):
-        for k in (1, 3, 2):
-            qy(h, k, 1).wait_recv()
-        for d in range(2):
-            qz(h, d, 1, 0, False).start()
-        step(h, 1, first=True)
-
+                qz(h, d, s, e, 1, False).wait_recv()
+                qz(h, d, s + 1, e, 0, last).start()
+
+    def steps(h, low, high):
         def body(s, carry):
             step(h, s)
             return carry
 
-        lax.fori_loop(2, far - 1, body, 0)
-        step(h, far - 1, last=True)
+        lax.fori_loop(low, high, body, 0)
+
+    def final(h):
         for d in range(2):
             pz(h, d, far, 1, True).wait_recv()
         spread(h, far, far)
         for d in range(2):
             relay(h, slot_of(d, far - 1), -sign[d] * (far - 1))
-        if h + 1 < H:
-            begin(h + 1)
-        for d in range(2):
-            qz(h, d, far, 1, True).wait_recv()
+
+    def tail(h):
+        for e in order:
+            for d in range(2):
+                qz(h, d, far, e, 1, True).wait_recv()
         relay(h, far, far)
 
         def rest(i, carry):
@@ -186,16 +205,8 @@
         ref = buf.at[lax.rem(me - back * k + n, n)]
         return remote(ref, ref, ss.at[k], rs.at[k], dev)
 
-    begin(0)
-    for k in range(1, nc):
-        b_copy(k, 0).start()
-    for h in range(H):
-        gather(h)
-        if h == 0:
-            for k in range(1, nc):
-                b_copy(k, 1).wait_recv()
-
-        def product(i, carry):
+    def product(h, low, high):
+        def body(i, carry):
             cols = pl.ds(pl.multiple_of(i * 2 * OCC, 2 * OCC), 2 * OCC)
             part = lax.dot_general(
                 A[h, :, cols], B[...], (((0,), (0,)), ((), ())), preferred_element_type=jnp.float32
@@ -203,7 +214,9 @@
             L[pl.ds(h * oh + 2 * i, 2)] = part.reshape(2, OCC, n_dev)
             return carry
 
-        lax.fori_loop(0, oh // 2, product, 0)
+        lax.fori_loop(low, high, body, 0)
+
+    def exchange(h):
         for k in range(1, nc):
             x_copy(h, k, 0).start()
         own = pltpu.make_async_copy(
@@ -213,6 +226,33 @@
         )
         own.start()
         own.wait()
+
+    begin(0)
+    for k in range(1, nc):
+        b_copy(k, 0).start()
+    join(0)
+    step(0, 1, first=True)
+    steps(0, 2, far - 2)
+    begin(1)
+    step(0, far - 2)
+    join(1)
+    step(0, far - 1, last=True)
+    step(1, 1, first=True)
+    final(0)
+    step(1, 2)
+    tail(0)
+    for k in range(1, nc):
+        b_copy(k, 1).wait_recv()
+    product(0, 0, oh // 4)
+    step(1, 3)
+    product(0, oh // 4, oh // 2)
+    exchange(0)
+    steps(1, 4, far - 1)
+    step(1, far - 1, last=True)
+    final(1)
+    tail(1)
+    product(1, 0, oh // 2)
+    exchange(1)
 
     for h in range(H):
         for k in range(1, nc):
@@ -258,12 +298,14 @@
         for d in range(2):
             def sent(s, carry):
                 pz(h, d, s, 0, False).wait_send()
-                qz(h, d, s, 0, False).wait_send()
+                for e in range(Y):
+                    qz(h, d, s, e, 0, False).wait_send()
                 return carry
 
             lax.fori_loop(1, far, sent, 0)
             pz(h, d, far, 0, True).wait_send()
-            qz(h, d, far, 0, True).wait_send()
+            for e in range(Y):
+                qz(h, d, far, e, 0, True).wait_send()
 
         def sent_y(i, carry):
             dz = jnp.where(i <= far, -i, i - far)
@@ -292,7 +334,7 @@
     occ = m_dev // OCC
     far = nz // 2
     dma = pltpu.SemaphoreType.DMA
-    pairs = [(H, 2, far + 1), (H, 2, far + 1), (H, nz, 4), (H, Y), (nc,), (H, nc), (nz,), (Y,)]
+    pairs = [(H, 2, far + 1), (H, 2, far + 1, Y), (H, nz, 4), (H, Y), (nc,), (H, nc), (nz,), (Y,)]
     summed, norm = pl.pallas_call(
         functools.partial(kernel, nz, nc),
         out_shape=(
@@ -300,11 +342,8 @@
             jax.ShapeDtypeStruct((occ, OCC), jnp.float32),
         ),
         in_specs=[
-            pl.BlockSpec(memory_space=pltpu.SMEM),
-            pl.BlockSpec(memory_space=pltpu.SMEM),
-            pl.BlockSpec(memory_space=pltpu.VMEM),
-            pl.BlockSpec(memory_space=pltpu.VMEM),
-        ],
+            pl.BlockSpec(memory_space=pl.ANY),
+        ] * 4,
         out_specs=(
             pl.BlockSpec(memory_space=pltpu.VMEM),
             pl.BlockSpec(memory_space=pltpu.VMEM),
@@ -316,10 +355,15 @@
             pltpu.VMEM((nc, occ, occ, n_dev), jnp.float32),
             pltpu.VMEM((nz, occ, OCC), jnp.float32),
             pltpu.VMEM((Y, occ, OCC), jnp.float32),
+            pltpu.VMEM((kb, m_dev), jnp.bfloat16),
+            pltpu.VMEM((kc, n_dev), jnp.bfloat16),
+            pltpu.SMEM((8, amp_mask.shape[1]), jnp.int32),
+            pltpu.SMEM((kc // kb, int_mask.shape[1]), jnp.int32),
+            dma((4,)),
             dma((H,)),
         ] + [dma(p) for p in pairs for _ in range(2)],
         compiler_params=pltpu.CompilerParams(
-            collective_id=0, has_side_effects=True, vmem_limit_bytes=40 << 20,
+            collective_id=0, has_side_effects=True, vmem_limit_bytes=60 << 20,
         ),
     )(amp_mask, int_mask, amplitudes, integrals)
     return summed.reshape(m_dev, n_dev) / norm.reshape(m_dev)[:, None], norm.reshape(m_dev)

time: 137 us -> 119 us (0.87)
  Pallas kernels: 130 us -> 114 us
  local copies, waits for them, and re-layouts: 3.91 us -> 0.6 us
  other arithmetic: 1.66 us -> 3.26 us
    pallas_call x1, Pallas kernels: 130 us -> 114 us  [local(): pl.pallas_call(functools.partial(kernel, nz, nc), out_shape=(jax.ShapeDty...]
    unnamed x9 -> x3, local copies, waits for them, and re-layouts: 3.91 us -> 0.6 us
    div x1, other arithmetic: 1.66 us -> 3.26 us  [local(): summed.reshape(m_dev, n_dev) / norm.reshape(m_dev)[:, None]]
where the time goes in v2:
time: 119 us; the launch traced here: 118 us
  Pallas kernels  114 us (96%)
  other arithmetic  3.26 us (3%)
    pallas_call x1, Pallas kernels, local(): pl.pallas_call(functools.partial(kernel, nz, nc), out_shape=(jax.ShapeDty...  114 us
    div x1, other arithmetic, local(): summed.reshape(m_dev, n_dev) / norm.reshape(m_dev)[:, None]  3.26 us

profile of v2, /device:TPU:1, one launch (start us, length us, event | category | flops | bytes accessed | tf_op | source)
XLA Modules:
  0.0 118.3 jit_solution(17522834011587246871)
XLA Ops:
  0.6 113.8 %shard_map.59 = (f32[16,128,256]{2,1,0:T(8,128)}, f32[16,128]{1,0:T(8,128)}) custom-call(s32[64,128]{1,0:T(8,128)} %am_ref.1, s32[64,128]{1,0:T(8,128)} %bm_ref.1, bf16[32,2048]{1,0:T(8,128)(2,1)} %a_ref.1, bf16[256,256]{1,0:T(8,128)(2,1)} %b_ref.1), custom_call_target="tpu_custom_call" | custom-call | tf_op jit(solution)/shard_map/pallas_call | solution.py:338
  114.5 0.0 copy-start
  114.5 3.3 %bitcast_divide_fusion = f32[2048,256]{1,0:T(8,128)} fusion(f32[16,128,256]{2,1,0:T(8,128)} %get-tuple-element.4, f32[2048]{0:T(1024)} %bitcast.3), kind=kLoop, calls=%fused_computation | loop fusion | flops 524288 | bytes 4202496 | tf_op jit(solution)/shard_map/div | solution.py:369
  117.7 0.0 copy-done
  117.7 0.6 copy.7
Async XLA Ops:
  114.5 3.3 %copy-start = (f32[16,128]{1,0:T(8,128)S(1)}, f32[16,128]{1,0:T(8,128)}, u32[]{:S(2)}) copy-start(f32[16,128]{1,0:T(8,128)} %get-tuple-element.5) | copy-start | bytes 24580

commit v3 on v2

--- a/solution.py
+++ b/solution.py
@@ -11,13 +11,15 @@
 OCC = 128
 Y = 4
 H = 2
+CUTS = ((0, 8), (8, 16))
+PART = (5, 5)
 MESH = pl.DeviceIdType.MESH
 WIDTH = 16384
 
 
 def kernel(
-    nz, nc, am_ref, bm_ref, a_ref, b_ref, s_ref, n_ref,
-    A, B, L, R, NZ, NY,
+    nz, nc, am_ref, bm_ref, a_ref, b_ref, out_ref, n_ref,
+    A, B, L, R, NZ, NY, s_ref, out_sem,
     a_own, b_own, am_own, bm_own, in_sem,
     loc_sem,
     pz_s, pz_r, qz_s, qz_r, py_s, py_r, qy_s, qy_r,
@@ -25,11 +27,13 @@
 ):
     kb, m_dev = a_ref.shape
     kc, n_dev = b_ref.shape
-    mh = m_dev // H
-    cp = (mh * 5 // 8) // TILE * TILE
     half = kb // 2
     occ = m_dev // OCC
-    oh = occ // H
+    start_of = [a * occ // 16 for a, b in CUTS]
+    count_of = [(b - a) * occ // 16 for a, b in CUTS]
+    low = [a * OCC for a in start_of]
+    mid = [low[h] + PART[h] * m_dev // 16 for h in range(H)]
+    high = [low[h] + count_of[h] * OCC for h in range(H)]
     far = nz // 2
     r = lax.axis_index("row")
     c = lax.axis_index("col")
@@ -74,7 +78,7 @@
         keep = am_own[r % 8, c * (m_dev // TILE) + t].astype(jnp.float32)
         lo = t * TILE
         val = (a_own[:, lo:lo + TILE].astype(jnp.float32) * keep).astype(jnp.bfloat16)
-        A[lo // mh, pl.ds(pl.multiple_of(r * kb, kb), kb), lo % mh:lo % mh + TILE] = val
+        A[pl.ds(pl.multiple_of(r * kb, kb), kb), lo:lo + TILE] = val
     for u in range(kc // kb):
         for t in range(n_dev // TILE):
             keep = bm_own[u, r * (n_dev // TILE) + t].astype(jnp.float32)
@@ -85,12 +89,12 @@
     def block(h, dz, dy, first, rows):
         zz = lax.rem(z + dz + 2 * nz, nz)
         yy = lax.rem(y + dy + 2 * Y, Y)
-        return A.at[h, pl.ds(pl.multiple_of((zz * Y + yy) * kb + first, half), rows), :cp]
+        return A.at[pl.ds(pl.multiple_of((zz * Y + yy) * kb + first, half), rows), low[h]:mid[h]]
 
     def rest_of(h, dz, dy, first, rows):
         zz = lax.rem(z + dz + 2 * nz, nz)
         yy = lax.rem(y + dy + 2 * Y, Y)
-        return A.at[h, pl.ds(pl.multiple_of((zz * Y + yy) * kb + first, half), rows), cp:]
+        return A.at[pl.ds(pl.multiple_of((zz * Y + yy) * kb + first, half), rows), mid[h]:high[h]]
 
     sign = (1, -1)
 
@@ -159,12 +163,12 @@
                 qz(h, d, s, e, 1, False).wait_recv()
                 qz(h, d, s + 1, e, 0, last).start()
 
-    def steps(h, low, high):
+    def steps(h, begin_at, end_at):
         def body(s, carry):
             step(h, s)
             return carry
 
-        lax.fori_loop(low, high, body, 0)
+        lax.fori_loop(begin_at, end_at, body, 0)
 
     def final(h):
         for d in range(2):
@@ -196,8 +200,8 @@
         to = lax.rem(c + (1 - back) * k, nc)
         src = lax.rem(c - back * k + nc, nc)
         return remote(
-            L.at[pl.ds(h * oh, oh), pl.ds(pl.multiple_of(to * occ, occ), occ), :],
-            R.at[src, pl.ds(h * oh, oh)],
+            L.at[pl.ds(start_of[h], count_of[h]), pl.ds(pl.multiple_of(to * occ, occ), occ), :],
+            R.at[src, pl.ds(start_of[h], count_of[h])],
             x_s.at[h, k], x_r.at[h, k], at_c(k),
         )
 
@@ -205,23 +209,23 @@
         ref = buf.at[lax.rem(me - back * k + n, n)]
         return remote(ref, ref, ss.at[k], rs.at[k], dev)
 
-    def product(h, low, high):
+    def product(h, begin_at, end_at):
         def body(i, carry):
-            cols = pl.ds(pl.multiple_of(i * 2 * OCC, 2 * OCC), 2 * OCC)
+            cols = pl.ds(pl.multiple_of(low[h] + i * 2 * OCC, 2 * OCC), 2 * OCC)
             part = lax.dot_general(
-                A[h, :, cols], B[...], (((0,), (0,)), ((), ())), preferred_element_type=jnp.float32
+                A[:, cols], B[...], (((0,), (0,)), ((), ())), preferred_element_type=jnp.float32
             )
-            L[pl.ds(h * oh + 2 * i, 2)] = part.reshape(2, OCC, n_dev)
-            return carry
-
-        lax.fori_loop(low, high, body, 0)
+            L[pl.ds(start_of[h] + 2 * i, 2)] = part.reshape(2, OCC, n_dev)
+            return carry
+
+        lax.fori_loop(begin_at, end_at, body, 0)
 
     def exchange(h):
         for k in range(1, nc):
             x_copy(h, k, 0).start()
         own = pltpu.make_async_copy(
-            L.at[pl.ds(h * oh, oh), pl.ds(pl.multiple_of(c * occ, occ), occ), :],
-            R.at[c, pl.ds(h * oh, oh)],
+            L.at[pl.ds(start_of[h], count_of[h]), pl.ds(pl.multiple_of(c * occ, occ), occ), :],
+            R.at[c, pl.ds(start_of[h], count_of[h])],
             loc_sem.at[h],
         )
         own.start()
@@ -232,40 +236,50 @@
         b_copy(k, 0).start()
     join(0)
     step(0, 1, first=True)
-    steps(0, 2, far - 2)
+    steps(0, 2, 4)
     begin(1)
-    step(0, far - 2)
+    step(0, 4)
     join(1)
+    step(0, 5)
+    step(1, 1, first=True)
+    step(0, 6)
+    step(1, 2)
     step(0, far - 1, last=True)
-    step(1, 1, first=True)
+    step(1, 3)
     final(0)
-    step(1, 2)
+    step(1, 4)
     tail(0)
     for k in range(1, nc):
         b_copy(k, 1).wait_recv()
-    product(0, 0, oh // 4)
-    step(1, 3)
-    product(0, oh // 4, oh // 2)
+    product(0, 0, count_of[0] // 4)
+    step(1, 5)
+    product(0, count_of[0] // 4, count_of[0] // 2)
     exchange(0)
-    steps(1, 4, far - 1)
+    steps(1, 6, far - 1)
     step(1, far - 1, last=True)
     final(1)
     tail(1)
-    product(1, 0, oh // 2)
+    product(1, 0, count_of[1] // 2)
     exchange(1)
 
+    done = 0
     for h in range(H):
         for k in range(1, nc):
             x_copy(h, k, 1).wait_recv()
+        ready = (start_of[h] + count_of[h]) // 8 * 8
 
         def add(src, carry):
-            for o in range(0, oh, 8):
-                got = jnp.swapaxes(R[src, pl.ds(h * oh + o, 8)], 0, 1)
-                at = pl.ds(pl.multiple_of(src * occ + h * oh + o, 8), 8)
+            for o in range(done, ready, 8):
+                got = jnp.swapaxes(R[src, pl.ds(o, 8)], 0, 1)
+                at = pl.ds(pl.multiple_of(src * occ + o, 8), 8)
                 s_ref[:, at, :] = L[:, at, :] + got
             return carry
 
         lax.fori_loop(0, nc, add, 0)
+        done = ready
+
+    out = pltpu.make_async_copy(s_ref, out_ref, out_sem)
+    out.start()
 
     def squares(i, carry):
         v = s_ref[i]
@@ -279,6 +293,34 @@
     lax.fori_loop(0, occ, squares, 0)
     for k in range(1, nz):
         n_copy(NZ, nz_s, nz_r, z, k, nz, at_z(k), 0).start()
+
+    for h in range(H):
+        for d in range(2):
+            def sent(s, carry):
+                pz(h, d, s, 0, False).wait_send()
+                for e in range(Y):
+                    qz(h, d, s, e, 0, False).wait_send()
+                return carry
+
+            lax.fori_loop(1, far, sent, 0)
+            pz(h, d, far, 0, True).wait_send()
+            for e in range(Y):
+                qz(h, d, far, e, 0, True).wait_send()
+
+        def sent_y(i, carry):
+            dz = jnp.where(i <= far, -i, i - far)
+            for kind in range(4):
+                py(h, i, dz, kind, 0).wait_send()
+            return carry
+
+        lax.fori_loop(0, nz, sent_y, 0)
+        for k in range(1, Y):
+            qy(h, k, 0).wait_send()
+        for k in range(1, nc):
+            x_copy(h, k, 0).wait_send()
+    for k in range(1, nc):
+        b_copy(k, 0).wait_send()
+
     for k in range(1, nz):
         n_copy(NZ, nz_s, nz_r, z, k, nz, at_z(k), 1).wait_recv()
     total = NZ[0]
@@ -293,37 +335,11 @@
     for q in range(1, Y):
         total = total + NY[q]
     n_ref[...] = jnp.sqrt(total / WIDTH + 1e-06)
-
-    for h in range(H):
-        for d in range(2):
-            def sent(s, carry):
-                pz(h, d, s, 0, False).wait_send()
-                for e in range(Y):
-                    qz(h, d, s, e, 0, False).wait_send()
-                return carry
-
-            lax.fori_loop(1, far, sent, 0)
-            pz(h, d, far, 0, True).wait_send()
-            for e in range(Y):
-                qz(h, d, far, e, 0, True).wait_send()
-
-        def sent_y(i, carry):
-            dz = jnp.where(i <= far, -i, i - far)
-            for kind in range(4):
-                py(h, i, dz, kind, 0).wait_send()
-            return carry
-
-        lax.fori_loop(0, nz, sent_y, 0)
-        for k in range(1, Y):
-            qy(h, k, 0).wait_send()
-        for k in range(1, nc):
-            x_copy(h, k, 0).wait_send()
-    for k in range(1, nc):
-        b_copy(k, 0).wait_send()
     for k in range(1, nz):
         n_copy(NZ, nz_s, nz_r, z, k, nz, at_z(k), 0).wait_send()
     for k in range(1, Y):
         n_copy(NY, ny_s, ny_r, y, k, Y, at_y(k), 0).wait_send()
+    out.wait()
 
 
 def local(nrow, nc, amplitudes, integrals, amp_mask, int_mask):
@@ -345,16 +361,18 @@
             pl.BlockSpec(memory_space=pl.ANY),
         ] * 4,
         out_specs=(
-            pl.BlockSpec(memory_space=pltpu.VMEM),
+            pl.BlockSpec(memory_space=pl.ANY),
             pl.BlockSpec(memory_space=pltpu.VMEM),
         ),
         scratch_shapes=[
-            pltpu.VMEM((H, k_all, m_dev // H), jnp.bfloat16),
+            pltpu.VMEM((k_all, m_dev), jnp.bfloat16),
             pltpu.VMEM((k_all, n_dev), jnp.bfloat16),
             pltpu.VMEM((occ, OCC, n_dev), jnp.float32),
             pltpu.VMEM((nc, occ, occ, n_dev), jnp.float32),
             pltpu.VMEM((nz, occ, OCC), jnp.float32),
             pltpu.VMEM((Y, occ, OCC), jnp.float32),
+            pltpu.VMEM((occ, OCC, n_dev), jnp.float32),
+            dma,
             pltpu.VMEM((kb, m_dev), jnp.bfloat16),
             pltpu.VMEM((kc, n_dev), jnp.bfloat16),
             pltpu.SMEM((8, amp_mask.shape[1]), jnp.int32),

time: 119 us -> 116 us (0.975)
  Pallas kernels: 114 us -> 111 us
    pallas_call x1, Pallas kernels: 114 us -> 111 us  [local(): pl.pallas_call(functools.partial(kernel, nz, nc), out_shape=(jax.ShapeDty...]
where the time goes in v3:
time: 116 us
  Pallas kernels  111 us (96%)
  other arithmetic  3.26 us (3%)
    pallas_call x1, Pallas kernels, local(): pl.pallas_call(functools.partial(kernel, nz, nc), out_shape=(jax.ShapeDty...  111 us
    div x1, other arithmetic, local(): summed.reshape(m_dev, n_dev) / norm.reshape(m_dev)[:, None]  3.26 us

profile of v3, /device:TPU:1, one launch (start us, length us, event | category | flops | bytes accessed | tf_op | source)
XLA Modules:
  0.0 115.9 jit_solution(4435526702347928060)
XLA Ops:
  0.6 111.4 %shard_map.59 = (f32[16,128,256]{2,1,0:T(8,128)}, f32[16,128]{1,0:T(8,128)}) custom-call(s32[64,128]{1,0:T(8,128)} %am_ref.1, s32[64,128]{1,0:T(8,128)} %bm_ref.1, bf16[32,2048]{1,0:T(8,128)(2,1)} %a_ref.1, bf16[256,256]{1,0:T(8,128)(2,1)} %b_ref.1), custom_call_target="tpu_custom_call" | custom-call | tf_op jit(solution)/shard_map/pallas_call | solution.py:354
  112.0 0.0 copy-start
  112.0 3.3 %bitcast_divide_fusion = f32[2048,256]{1,0:T(8,128)} fusion(f32[16,128,256]{2,1,0:T(8,128)} %get-tuple-element.4, f32[2048]{0:T(1024)} %bitcast.3), kind=kLoop, calls=%fused_computation | loop fusion | flops 524288 | bytes 4202496 | tf_op jit(solution)/shard_map/div | solution.py:387
  115.3 0.0 copy-done
  115.3 0.6 copy.7
Async XLA Ops:
  112.0 3.3 %copy-start = (f32[16,128]{1,0:T(8,128)S(1)}, f32[16,128]{1,0:T(8,128)}, u32[]{:S(2)}) copy-start(f32[16,128]{1,0:T(8,128)} %get-tuple-element.5) | copy-start | bytes 24580
